TPU v7x, 32 devices: a whole 2x2x4 slice. The times are simulated.
32 devices in a mesh: blk: 4 (over y, x), inner: 8 (over z, core).
Axes of the slice: x: 2, y: 2, z: 4, core: 2. Of those that a mesh axis runs over, the one named last changes fastest.
Arguments:
- points: float32 [4096, 128], P(('blk', 'inner')), may hold values from -8 to 8
- lengthscales: float32 [128], replicated, may hold values from 6 to 24
- noise_level: float32 [1], replicated, may hold values from 1 to 10
- iterate: float32 [4096, 64], P(('blk', 'inner')), may hold values from -6 to 6
- residual: float32 [4096, 64], P(('blk', 'inner')), may hold values from -6 to 6
- direction: float32 [4096, 64], P(('blk', 'inner')), may hold values from -6 to 6
Outputs:
- new_iterate: float32 [4096, 64], P(('blk', 'inner'))
- new_residual: float32 [4096, 64], P(('blk', 'inner'))
- new_direction: float32 [4096, 64], P(('blk', 'inner'))
All inputs are finite; a program needn't handle non-finite values.
Results may differ from a plain program's by a relative error of at most 0.00014.
Values sent between devices are 32-bit elements; how exact they have to be, the bound alone decides.
A program may use at most 64 MiB of HBM per device.

v0:
```python
import jax
import jax.numpy as jnp
from jax import lax
from jax.sharding import PartitionSpec as P


def from_behind(value, axis, by):
    size = lax.axis_size(axis)
    return lax.ppermute(value, axis, [(i, (i + by) % size) for i in range(size)])


def kernel_block(left, left_sq, right, right_sq):
    products = lax.dot_general(
        left,
        right,
        (((1,), (1,)), ((), ())),
        precision=lax.Precision.HIGHEST,
        preferred_element_type=jnp.float32,
    )
    return jnp.exp(-0.5 * (left_sq[:, None] + right_sq[None, :] - 2.0 * products))


def matmul(left, right):
    return jnp.dot(left, right, precision=lax.Precision.HIGHEST, preferred_element_type=jnp.float32)


def transposed(left, right):
    return lax.dot_general(
        left,
        right,
        (((0,), (0,)), ((), ())),
        precision=lax.Precision.HIGHEST,
        preferred_element_type=jnp.float32,
    )


def chol_solve(matrix, rhs_side):
    factor = jnp.linalg.cholesky(matrix)
    return jax.scipy.linalg.cho_solve((factor, True), rhs_side)


def on_device(points, lengthscales, noise_level, iterate, residual, direction):
    scaled = points / lengthscales[None, :]
    sq_norms = jnp.sum(scaled * scaled, axis=1)
    cycle_size = lax.axis_size("blk")
    group_pts, group_dir = (
        lax.all_gather(scaled, "inner", axis=0, tiled=True),
        lax.all_gather(direction, "inner", axis=0, tiled=True),
    )
    group_sq = jnp.sum(group_pts * group_pts, axis=1)
    partial_value = jnp.zeros((group_pts.shape[0], direction.shape[1]), jnp.float32)
    halfway = cycle_size // 2
    visitor = (scaled, sq_norms, direction, jnp.zeros_like(direction))
    returned = jnp.zeros_like(direction)
    for offset in range(halfway + 1):
        if offset > 0:
            visitor = from_behind((visitor[0], visitor[1], visitor[2], visitor[3]), "blk", 1)
        kernel_tile = kernel_block(group_pts, group_sq, visitor[0], visitor[1])
        partial_value = partial_value + matmul(kernel_tile, visitor[2])
        if 1 <= offset <= halfway - 1:
            carried = visitor[3] + transposed(kernel_tile, group_dir)
            visitor = (visitor[0], visitor[1], visitor[2], carried)
            if offset == halfway - 1:
                returned = from_behind(carried, "blk", -(halfway - 1))
    owned = lax.psum_scatter(partial_value, "inner", scatter_dimension=0, tiled=True)
    image = owned + returned + noise_level[0] * direction
    local_gram = transposed(direction, image)
    local_res = transposed(residual, residual)
    gram_raw, res_gram = lax.psum((local_gram, local_res), ("blk", "inner"))
    gram_matrix = 0.5 * (gram_raw + gram_raw.T)
    step_size = chol_solve(gram_matrix, res_gram)
    new_residual = residual - matmul(image, step_size)
    new_gram = lax.psum(transposed(new_residual, new_residual), ("blk", "inner"))
    new_iterate = iterate + matmul(direction, step_size)
    correction = chol_solve(res_gram, new_gram)
    new_direction = new_residual + matmul(direction, correction)
    return (new_iterate, new_residual, new_direction)


def solution(mesh):
    return jax.shard_map(
        on_device,
        mesh=mesh,
        in_specs=(
            P(("blk", "inner"), None),
            P(),
            P(),
            P(("blk", "inner"), None),
            P(("blk", "inner"), None),
            P(("blk", "inner"), None),
        ),
        out_specs=(P(("blk", "inner"), None), P(("blk", "inner"), None), P(("blk", "inner"), None)),
        check_vma=False,
    )
```

profile of v0, /device:TPU:0, one launch (start us, length us, event | category | flops | bytes accessed | tf_op | source)
XLA Modules:
  0.0 187.7 jit_solution(3288486812774204959)
XLA Ops:
  7.2 3.0 %collective-permute-start.6 = (f32[128,64]{0,1:T(8,128)S(1)}, f32[128,64]{0,1:T(8,128)S(1)}, u32[]{:S(2)}, u32[]{:S(2)}) collective-permute-start(f32[128,64]{0,1:T(8,128)S(1)} %broadcast_in_dim.2), channel_id=1, source_target_pairs={{0,8},{8,16},{16,24},{24,0},{1,9},{9,17},{17,25},{25,1},{2,10},{10... | collective-permute-start | bytes 98312 | tf_op jit(solution)/shard_map/ppermute | solution.py:9
  10.3 1.5 collective-permute-start.2
  11.8 0.9 multiply_reduce_fusion.1
  12.7 1.5 collective-permute-start
  14.9 15.0 %all_gather.6 = f32[1024,128]{1,0:T(8,128)S(1)} all-gather(f32[128,128]{1,0:T(8,128)S(1)} %get-tuple-element.8), channel_id=1, replica_groups=mesh['blk'=4,'inner'=8] {'inner'}, dimensions={0}, use_global_device_ids=true | all-gather | bytes 589824 | tf_op jit(solution)/shard_map/all_gather | solution.py:47
  31.4 1.4 collective-permute-start.3
  32.8 1.5 collective-permute-start.5
  34.3 1.5 collective-permute-start.4
  36.4 0.9 convolution_add_fusion.1
  37.3 2.2 %collective-permute-done.4 = f32[128,128]{1,0:T(8,128)S(1)} collective-permute-done((f32[128,128]{1,0:T(8,128)S(1)}, f32[128,128]{1,0:T(8,128)S(1)}, u32[]{:S(2)}, u32[]{:S(2)}) %collective-permute-start.4) | collective-permute-done | bytes 65568 | tf_op jit(solution)/shard_map/ppermute | solution.py:9
  40.1 1.6 convolution_add_fusion
  41.7 14.3 %all_gather.7 = f32[1024,64]{0,1:T(8,128)S(1)} all-gather(f32[128,64]{0,1:T(8,128)S(1)} %copy-done), channel_id=1, replica_groups=mesh['blk'=4,'inner'=8] {'inner'}, dimensions={0}, use_global_device_ids=true | all-gather | bytes 294912 | tf_op jit(solution)/shard_map/all_gather | solution.py:48
  56.5 0.8 collective-permute-start.7
  58.2 2.3 %collective-permute-done.7 = f32[128,64]{0,1:T(8,128)S(1)} collective-permute-done((f32[128,64]{0,1:T(8,128)S(1)}, f32[128,64]{0,1:T(8,128)S(1)}, u32[]{:S(2)}, u32[]{:S(2)}) %collective-permute-start.7) | collective-permute-done | bytes 32800 | tf_op jit(solution)/shard_map/ppermute | solution.py:9
  60.5 11.5 %reduce-scatter.2.cloned.1.call-done = f32[128,64]{0,1:T(8,128)} async-done(((f32[1024,64]{0,1:T(8,128)}), f32[128,64]{0,1:T(8,128)}) %reduce-scatter.2.cloned.1.call-update) | async-done | bytes 32784 | tf_op jit(solution)/shard_map/reduce_scatter | solution.py:65
  72.0 0.9 convolution_bitcast_fusion.2
  73.0 38.3 %all-reduce = (f32[64,64]{0,1:T(8,128)S(1)}, f32[64,64]{1,0:T(8,128)S(1)}) all-reduce(f32[64,64]{0,1:T(8,128)S(1)} %fusion.35, f32[64,64]{1,0:T(8,128)S(1)} %convolution_bitcast_fusion.2), channel_id=1, replica_groups=mesh['blk'=4,'inner'=8] {'blk','inner'}, use_global_device_ids=true, to_apply=%region_6.8 | all-reduce | flops 8192 | bytes 65536 | tf_op jit(solution)/shard_map/psum | solution.py:69
  111.5 5.8 %cholesky.44 = f32[64,64]{1,0:T(8,128)S(1)} custom-call(f32[64,64]{1,0:T(8,128)S(1)} %fusion.29), custom_call_target="Cholesky" | custom-call | tf_op jit(solution)/shard_map/jit(cholesky)/cholesky | solution.py:38
  118.6 4.9 %custom-call.8 = f32[1,64,64]{1,2,0:T(8,128)S(1)} custom-call(f32[1,64,64]{2,1,0:T(8,128)S(1)} %fusion.18), custom_call_target="InvertDiagBlocksLowerTriangular" | custom-call | tf_op jit(solution)/shard_map/jit(_cho_solve)/triangular_solve | solution.py:39
  124.6 0.9 fusion.4
  125.9 41.5 %psum.23 = f32[64,64]{1,0:T(8,128)S(1)} all-reduce(f32[64,64]{1,0:T(8,128)S(1)} %fusion.36), channel_id=1, replica_groups=mesh['blk'=4,'inner'=8] {'blk','inner'}, use_global_device_ids=true, to_apply=%region_7.10 | all-reduce | flops 4096 | bytes 32768 | tf_op jit(solution)/shard_map/psum | solution.py:73
  167.5 5.8 %cholesky.55 = f32[64,64]{1,0:T(8,128)S(1)} custom-call(f32[64,64]{1,0:T(8,128)S(1)} %fusion.24), custom_call_target="Cholesky" | custom-call | tf_op jit(solution)/shard_map/jit(cholesky)/cholesky | solution.py:38
  174.7 4.9 %custom-call.9 = f32[1,64,64]{1,2,0:T(8,128)S(1)} custom-call(f32[1,64,64]{2,1,0:T(8,128)S(1)} %fusion.19), custom_call_target="InvertDiagBlocksLowerTriangular" | custom-call | tf_op jit(solution)/shard_map/jit(_cho_solve)/triangular_solve | solution.py:39
  180.0 0.9 fusion.3
  (47 shorter events, 8.9 us)
Async XLA Ops:
  7.2 3.1 %copy-start = (f32[128,64]{0,1:T(8,128)S(1)}, f32[128,64]{0,1:T(8,128)}, u32[]{:S(2)}) copy-start(f32[128,64]{0,1:T(8,128)} %param.14) | copy-start | bytes 98308
  7.2 4.6 %copy-start.5 = (f32[128]{0:T(128)S(1)}, f32[128]{0:T(128)}, u32[]{:S(2)}) copy-start(f32[128]{0:T(128)} %param.10) | copy-start | bytes 1540
  7.2 64.8 %reduce-scatter.2.cloned.1.call-start = ((), (), s32[]{:S(2)}) async-start(), calls=%async_computation.1 | async-start | bytes 294912 | tf_op jit(solution)/shard_map/reduce_scatter | solution.py:65
  7.2 48.7 %collective-permute-start.6 = (f32[128,64]{0,1:T(8,128)S(1)}, f32[128,64]{0,1:T(8,128)S(1)}, u32[]{:S(2)}, u32[]{:S(2)}) collective-permute-start(f32[128,64]{0,1:T(8,128)S(1)} %broadcast_in_dim.2), channel_id=1, source_target_pairs={{0,8},{8,16},{16,24},{24,0},{1,9},{9,17},{17,25},{25,1},{2,10},{10... | collective-permute-start | bytes 98312 | tf_op jit(solution)/shard_map/ppermute | solution.py:9
  10.3 22.6 %collective-permute-start.2 = (f32[128,64]{0,1:T(8,128)S(1)}, f32[128,64]{0,1:T(8,128)S(1)}, u32[]{:S(2)}, u32[]{:S(2)}) collective-permute-start(f32[128,64]{0,1:T(8,128)S(1)} %copy-done), channel_id=1, source_target_pairs={{0,8},{8,16},{16,24},{24,0},{1,9},{9,17},{17,25},{25,1},{2,10},{10... | collective-permute-start | bytes 98312 | tf_op jit(solution)/shard_map/ppermute | solution.py:9
  12.7 18.7 %collective-permute-start = (f32[128]{0:T(128)S(1)}, f32[128]{0:T(128)S(1)}, u32[]{:S(2)}, u32[]{:S(2)}) collective-permute-start(f32[128]{0:T(128)S(1)} %get-tuple-element.7), channel_id=1, source_target_pairs={{0,8},{8,16},{16,24},{24,0},{1,9},{9,17},{17,25},{25,1},{2,10},{10... | collective-permute-start | bytes 1544 | tf_op jit(solution)/shard_map/ppermute | solution.py:9
  14.3 20.1 %collective-permute-start.1 = (f32[128,128]{1,0:T(8,128)S(1)}, f32[128,128]{1,0:T(8,128)S(1)}, u32[]{:S(2)}, u32[]{:S(2)}) collective-permute-start(f32[128,128]{1,0:T(8,128)S(1)} %get-tuple-element.8), channel_id=1, source_target_pairs={{0,8},{8,16},{16,24},{24,0},{1,9},{9,17},{17,25},{25,1},{2,10},{10... | collective-permute-start | bytes 196616 | tf_op jit(solution)/shard_map/ppermute | solution.py:9
  31.4 8.6 %collective-permute-start.3 = (f32[128]{0:T(128)S(1)}, f32[128]{0:T(128)S(1)}, u32[]{:S(2)}, u32[]{:S(2)}) collective-permute-start(f32[128]{0:T(128)S(1)} %collective-permute-done), channel_id=1, source_target_pairs={{0,8},{8,16},{16,24},{24,0},{1,9},{9,17},{17,25},{25,1},{2,10},{10... | collective-permute-start | bytes 1544 | tf_op jit(solution)/shard_map/ppermute | solution.py:9
  32.8 7.3 %collective-permute-start.5 = (f32[128,64]{0,1:T(8,128)S(1)}, f32[128,64]{0,1:T(8,128)S(1)}, u32[]{:S(2)}, u32[]{:S(2)}) collective-permute-start(f32[128,64]{0,1:T(8,128)S(1)} %collective-permute-done.2), channel_id=1, source_target_pairs={{0,8},{8,16},{16,24},{24,0},{1,9},{9,17},{17,25},{25,1},{2,10},{10... | collective-permute-start | bytes 98312 | tf_op jit(solution)/shard_map/ppermute | solution.py:9
  34.3 5.2 %collective-permute-start.4 = (f32[128,128]{1,0:T(8,128)S(1)}, f32[128,128]{1,0:T(8,128)S(1)}, u32[]{:S(2)}, u32[]{:S(2)}) collective-permute-start(f32[128,128]{1,0:T(8,128)S(1)} %collective-permute-done.1), channel_id=1, source_target_pairs={{0,8},{8,16},{16,24},{24,0},{1,9},{9,17},{17,25},{25,1},{2,10},{10... | collective-permute-start | bytes 196616 | tf_op jit(solution)/shard_map/ppermute | solution.py:9
  55.9 1.4 copy-start.2
  56.5 4.0 %collective-permute-start.7 = (f32[128,64]{0,1:T(8,128)S(1)}, f32[128,64]{0,1:T(8,128)S(1)}, u32[]{:S(2)}, u32[]{:S(2)}) collective-permute-start(f32[128,64]{0,1:T(8,128)S(1)} %convolution_add_fusion.2), channel_id=1, source_target_pairs={{0,24},{8,0},{16,8},{24,16},{1,25},{9,1},{17,9},{25,17},{2,26},{10... | collective-permute-start | bytes 98312 | tf_op jit(solution)/shard_map/ppermute | solution.py:9
  123.9 0.8 copy-start.4
  124.6 0.9 copy-start.3
  125.7 54.3 %copy-start.1 = (f32[128,64]{0,1:T(8,128)}, f32[128,64]{0,1:T(8,128)S(1)}, u32[]{:S(2)}) copy-start(f32[128,64]{0,1:T(8,128)S(1)} %convolution_subtract_fusion) | copy-start | bytes 98308
Sparse Core Ops, SparseCore 0:
  41.8 30.1 reduce-scatter.1
where the time goes:
time: 188 us
  blocking collectives  109 us (58%)
  other arithmetic  25.3 us (13%)
  waiting for transfers between devices  16.1 us (9%)
  between operations  14.9 us (8%)
  starting transfers between devices  11.9 us (6%)
  matrix products  9.55 us (5%)
    psum x1, blocking collectives, on_device(): lax.psum(transposed(new_residual, new_residual), ('blk', 'inner'))  41.5 us
    psum x1, blocking collectives, on_device(): gram_raw, res_gram = lax.psum((local_gram, local_res), ('blk', 'inner'))  38.3 us
    all_gather x1, blocking collectives, on_device(): lax.all_gather(scaled, 'inner', axis=0, tiled=True)  15 us
    all_gather x1, blocking collectives, on_device(): lax.all_gather(direction, 'inner', axis=0, tiled=True)  14.3 us
    another operation x6, other arithmetic, chol_solve(): factor = jnp.linalg.cholesky(matrix)  13 us
    ppermute x8, starting transfers between devices, from_behind(): lax.ppermute(value, axis, [(i, (i + by) % size) for i in range(size)])  11.8 us
    reduce_scatter x1, waiting for transfers between devices, on_device(): lax.psum_scatter(partial_value, 'inner', scatter_dimension=0, tiled=True)  11.5 us
    another operation x4, other arithmetic, chol_solve(): return jax.scipy.linalg.cho_solve((factor, True), rhs_side)  11.1 us
  transfers between devices with their start and end apart: 9, of which 3 were waited for; matrix products, arithmetic and copies ran while one was open for 4% of the time, Pallas kernels for 0%

commit v1 on v0

--- a/solution.py
+++ b/solution.py
@@ -70,7 +70,9 @@
     gram_matrix = 0.5 * (gram_raw + gram_raw.T)
     step_size = chol_solve(gram_matrix, res_gram)
     new_residual = residual - matmul(image, step_size)
-    new_gram = lax.psum(transposed(new_residual, new_residual), ("blk", "inner"))
+    own = transposed(new_residual, new_residual)
+    parts = lax.all_gather(own, ("blk", "inner"), axis=0, tiled=False)
+    new_gram = parts.sum(axis=0)
     new_iterate = iterate + matmul(direction, step_size)
     correction = chol_solve(res_gram, new_gram)
     new_direction = new_residual + matmul(direction, correction)

time: 188 us -> 192 us (1.021)
  blocking collectives: 109 us -> 112 us
    all_gather x0 -> x1, blocking collectives: none -> 44.9 us  [on_device(): parts = lax.all_gather(own, ('blk', 'inner'), axis=0, tiled=False)]
    psum x1 -> x0, blocking collectives: 41.5 us -> none  [on_device(): lax.psum(transposed(new_residual, new_residual), ('blk', 'inner'))]
where the time goes in v1:
time: 192 us; the launch traced here: 191 us
  blocking collectives  112 us (58%)
  other arithmetic  25.4 us (13%)
  waiting for transfers between devices  16.2 us (8%)
  between operations  14.9 us (8%)
  starting transfers between devices  11.8 us (6%)
  matrix products  9.53 us (5%)
    all_gather x1, blocking collectives, on_device(): parts = lax.all_gather(own, ('blk', 'inner'), axis=0, tiled=False)  44.9 us
    psum x1, blocking collectives, on_device(): gram_raw, res_gram = lax.psum((local_gram, local_res), ('blk', 'inner'))  38.4 us
    all_gather x1, blocking collectives, on_device(): lax.all_gather(scaled, 'inner', axis=0, tiled=True)  15 us
    all_gather x1, blocking collectives, on_device(): lax.all_gather(direction, 'inner', axis=0, tiled=True)  14.2 us
    another operation x6, other arithmetic, chol_solve(): factor = jnp.linalg.cholesky(matrix)  13 us
    ppermute x8, starting transfers between devices, from_behind(): lax.ppermute(value, axis, [(i, (i + by) % size) for i in range(size)])  11.8 us
    reduce_scatter x1, waiting for transfers between devices, on_device(): lax.psum_scatter(partial_value, 'inner', scatter_dimension=0, tiled=True)  11.5 us
    another operation x4, other arithmetic, chol_solve(): return jax.scipy.linalg.cho_solve((factor, True), rhs_side)  11.1 us
  transfers between devices with their start and end apart: 9, of which 3 were waited for; matrix products, arithmetic and copies ran while one was open for 4% of the time, Pallas kernels for 0%

profile of v1, /device:TPU:0, one launch (start us, length us, event | category | flops | bytes accessed | tf_op | source)
XLA Modules:
  0.0 191.2 jit_solution(3578788799790931888)
XLA Ops:
  7.2 3.0 %collective-permute-start.6 = (f32[128,64]{0,1:T(8,128)S(1)}, f32[128,64]{0,1:T(8,128)S(1)}, u32[]{:S(2)}, u32[]{:S(2)}) collective-permute-start(f32[128,64]{0,1:T(8,128)S(1)} %broadcast_in_dim.2), channel_id=1, source_target_pairs={{0,8},{8,16},{16,24},{24,0},{1,9},{9,17},{17,25},{25,1},{2,10},{10... | collective-permute-start | bytes 98312 | tf_op jit(solution)/shard_map/ppermute | solution.py:9
  10.3 1.5 collective-permute-start.2
  11.8 0.9 multiply_reduce_fusion.1
  12.7 1.5 collective-permute-start
  14.9 15.0 %all_gather.12 = f32[1024,128]{1,0:T(8,128)S(1)} all-gather(f32[128,128]{1,0:T(8,128)S(1)} %get-tuple-element.8), channel_id=1, replica_groups=mesh['blk'=4,'inner'=8] {'inner'}, dimensions={0}, use_global_device_ids=true | all-gather | bytes 589824 | tf_op jit(solution)/shard_map/all_gather | solution.py:47
  31.4 1.4 collective-permute-start.3
  32.8 1.5 collective-permute-start.5
  34.3 1.5 collective-permute-start.4
  36.4 0.9 convolution_add_fusion.1
  37.3 2.2 %collective-permute-done.4 = f32[128,128]{1,0:T(8,128)S(1)} collective-permute-done((f32[128,128]{1,0:T(8,128)S(1)}, f32[128,128]{1,0:T(8,128)S(1)}, u32[]{:S(2)}, u32[]{:S(2)}) %collective-permute-start.4) | collective-permute-done | bytes 65568 | tf_op jit(solution)/shard_map/ppermute | solution.py:9
  40.1 1.6 convolution_add_fusion
  41.7 14.2 %all_gather.13 = f32[1024,64]{0,1:T(8,128)S(1)} all-gather(f32[128,64]{0,1:T(8,128)S(1)} %copy-done), channel_id=1, replica_groups=mesh['blk'=4,'inner'=8] {'inner'}, dimensions={0}, use_global_device_ids=true | all-gather | bytes 294912 | tf_op jit(solution)/shard_map/all_gather | solution.py:48
  56.5 0.7 collective-permute-start.7
  58.1 2.4 %collective-permute-done.7 = f32[128,64]{0,1:T(8,128)S(1)} collective-permute-done((f32[128,64]{0,1:T(8,128)S(1)}, f32[128,64]{0,1:T(8,128)S(1)}, u32[]{:S(2)}, u32[]{:S(2)}) %collective-permute-start.7) | collective-permute-done | bytes 32800 | tf_op jit(solution)/shard_map/ppermute | solution.py:9
  60.5 11.5 %reduce-scatter.2.cloned.1.call-done = f32[128,64]{0,1:T(8,128)} async-done(((f32[1024,64]{0,1:T(8,128)}), f32[128,64]{0,1:T(8,128)}) %reduce-scatter.2.cloned.1.call-update) | async-done | bytes 32784 | tf_op jit(solution)/shard_map/reduce_scatter | solution.py:65
  72.0 0.9 convolution_bitcast_fusion.2
  72.9 38.4 %all-reduce = (f32[64,64]{0,1:T(8,128)S(1)}, f32[64,64]{1,0:T(8,128)S(1)}) all-reduce(f32[64,64]{0,1:T(8,128)S(1)} %fusion.35, f32[64,64]{1,0:T(8,128)S(1)} %convolution_bitcast_fusion.2), channel_id=1, replica_groups=mesh['blk'=4,'inner'=8] {'blk','inner'}, use_global_device_ids=true, to_apply=%region_6.8 | all-reduce | flops 8192 | bytes 65536 | tf_op jit(solution)/shard_map/psum | solution.py:69
  111.5 5.8 %cholesky.44 = f32[64,64]{1,0:T(8,128)S(1)} custom-call(f32[64,64]{1,0:T(8,128)S(1)} %fusion.29), custom_call_target="Cholesky" | custom-call | tf_op jit(solution)/shard_map/jit(cholesky)/cholesky | solution.py:38
  118.7 4.9 %custom-call.8 = f32[1,64,64]{1,2,0:T(8,128)S(1)} custom-call(f32[1,64,64]{2,1,0:T(8,128)S(1)} %fusion.18), custom_call_target="InvertDiagBlocksLowerTriangular" | custom-call | tf_op jit(solution)/shard_map/jit(_cho_solve)/triangular_solve | solution.py:39
  124.7 0.9 fusion.4
  126.0 5.8 %cholesky.55 = f32[64,64]{1,0:T(8,128)S(1)} custom-call(f32[64,64]{1,0:T(8,128)S(1)} %fusion.24), custom_call_target="Cholesky" | custom-call | tf_op jit(solution)/shard_map/jit(cholesky)/cholesky | solution.py:38
  133.2 4.9 %custom-call.9 = f32[1,64,64]{1,2,0:T(8,128)S(1)} custom-call(f32[1,64,64]{2,1,0:T(8,128)S(1)} %fusion.19), custom_call_target="InvertDiagBlocksLowerTriangular" | custom-call | tf_op jit(solution)/shard_map/jit(_cho_solve)/triangular_solve | solution.py:39
  138.1 44.9 %all-gather = f32[2048,64]{1,0:T(8,128)S(1)} all-gather(f32[64,64]{1,0:T(8,128)S(1)} %fusion.36), channel_id=2, replica_groups=mesh['blk'=4,'inner'=8] {'blk','inner'}, dimensions={0}, use_global_device_ids=true | all-gather | bytes 540672 | tf_op jit(solution)/shard_map/all_gather | solution.py:74
  183.5 0.9 fusion.3
  (48 shorter events, 9.0 us)
Async XLA Ops:
  7.2 3.1 %copy-start = (f32[128,64]{0,1:T(8,128)S(1)}, f32[128,64]{0,1:T(8,128)}, u32[]{:S(2)}) copy-start(f32[128,64]{0,1:T(8,128)} %param.14) | copy-start | bytes 98308
  7.2 4.6 %copy-start.5 = (f32[128]{0:T(128)S(1)}, f32[128]{0:T(128)}, u32[]{:S(2)}) copy-start(f32[128]{0:T(128)} %param.10) | copy-start | bytes 1540
  7.2 64.8 %reduce-scatter.2.cloned.1.call-start = ((), (), s32[]{:S(2)}) async-start(), calls=%async_computation.1 | async-start | bytes 294912 | tf_op jit(solution)/shard_map/reduce_scatter | solution.py:65
  7.2 48.7 %collective-permute-start.6 = (f32[128,64]{0,1:T(8,128)S(1)}, f32[128,64]{0,1:T(8,128)S(1)}, u32[]{:S(2)}, u32[]{:S(2)}) collective-permute-start(f32[128,64]{0,1:T(8,128)S(1)} %broadcast_in_dim.2), channel_id=1, source_target_pairs={{0,8},{8,16},{16,24},{24,0},{1,9},{9,17},{17,25},{25,1},{2,10},{10... | collective-permute-start | bytes 98312 | tf_op jit(solution)/shard_map/ppermute | solution.py:9
  10.3 22.6 %collective-permute-start.2 = (f32[128,64]{0,1:T(8,128)S(1)}, f32[128,64]{0,1:T(8,128)S(1)}, u32[]{:S(2)}, u32[]{:S(2)}) collective-permute-start(f32[128,64]{0,1:T(8,128)S(1)} %copy-done), channel_id=1, source_target_pairs={{0,8},{8,16},{16,24},{24,0},{1,9},{9,17},{17,25},{25,1},{2,10},{10... | collective-permute-start | bytes 98312 | tf_op jit(solution)/shard_map/ppermute | solution.py:9
  12.7 18.7 %collective-permute-start = (f32[128]{0:T(128)S(1)}, f32[128]{0:T(128)S(1)}, u32[]{:S(2)}, u32[]{:S(2)}) collective-permute-start(f32[128]{0:T(128)S(1)} %get-tuple-element.7), channel_id=1, source_target_pairs={{0,8},{8,16},{16,24},{24,0},{1,9},{9,17},{17,25},{25,1},{2,10},{10... | collective-permute-start | bytes 1544 | tf_op jit(solution)/shard_map/ppermute | solution.py:9
  14.3 20.1 %collective-permute-start.1 = (f32[128,128]{1,0:T(8,128)S(1)}, f32[128,128]{1,0:T(8,128)S(1)}, u32[]{:S(2)}, u32[]{:S(2)}) collective-permute-start(f32[128,128]{1,0:T(8,128)S(1)} %get-tuple-element.8), channel_id=1, source_target_pairs={{0,8},{8,16},{16,24},{24,0},{1,9},{9,17},{17,25},{25,1},{2,10},{10... | collective-permute-start | bytes 196616 | tf_op jit(solution)/shard_map/ppermute | solution.py:9
  31.4 8.7 %collective-permute-start.3 = (f32[128]{0:T(128)S(1)}, f32[128]{0:T(128)S(1)}, u32[]{:S(2)}, u32[]{:S(2)}) collective-permute-start(f32[128]{0:T(128)S(1)} %collective-permute-done), channel_id=1, source_target_pairs={{0,8},{8,16},{16,24},{24,0},{1,9},{9,17},{17,25},{25,1},{2,10},{10... | collective-permute-start | bytes 1544 | tf_op jit(solution)/shard_map/ppermute | solution.py:9
  32.8 7.3 %collective-permute-start.5 = (f32[128,64]{0,1:T(8,128)S(1)}, f32[128,64]{0,1:T(8,128)S(1)}, u32[]{:S(2)}, u32[]{:S(2)}) collective-permute-start(f32[128,64]{0,1:T(8,128)S(1)} %collective-permute-done.2), channel_id=1, source_target_pairs={{0,8},{8,16},{16,24},{24,0},{1,9},{9,17},{17,25},{25,1},{2,10},{10... | collective-permute-start | bytes 98312 | tf_op jit(solution)/shard_map/ppermute | solution.py:9
  34.3 5.2 %collective-permute-start.4 = (f32[128,128]{1,0:T(8,128)S(1)}, f32[128,128]{1,0:T(8,128)S(1)}, u32[]{:S(2)}, u32[]{:S(2)}) collective-permute-start(f32[128,128]{1,0:T(8,128)S(1)} %collective-permute-done.1), channel_id=1, source_target_pairs={{0,8},{8,16},{16,24},{24,0},{1,9},{9,17},{17,25},{25,1},{2,10},{10... | collective-permute-start | bytes 196616 | tf_op jit(solution)/shard_map/ppermute | solution.py:9
  55.9 1.3 copy-start.2
  56.5 4.0 %collective-permute-start.7 = (f32[128,64]{0,1:T(8,128)S(1)}, f32[128,64]{0,1:T(8,128)S(1)}, u32[]{:S(2)}, u32[]{:S(2)}) collective-permute-start(f32[128,64]{0,1:T(8,128)S(1)} %convolution_add_fusion.2), channel_id=1, source_target_pairs={{0,24},{8,0},{16,8},{24,16},{1,25},{9,1},{17,9},{25,17},{2,26},{10... | collective-permute-start | bytes 98312 | tf_op jit(solution)/shard_map/ppermute | solution.py:9
  123.9 0.8 copy-start.4
  124.7 0.9 copy-start.3
  125.8 57.7 %copy-start.1 = (f32[128,64]{0,1:T(8,128)}, f32[128,64]{0,1:T(8,128)S(1)}, u32[]{:S(2)}) copy-start(f32[128,64]{0,1:T(8,128)S(1)} %convolution_subtract_fusion) | copy-start | bytes 98308
Sparse Core Ops, SparseCore 0:
  41.8 30.1 reduce-scatter.1
